TPU v7x, 32 devices: a whole 2x2x4 slice. The times are simulated.
32 devices in a mesh: dp: 32 (over z, y, x, core).
Axes of the slice: x: 2, y: 2, z: 4, core: 2. Of those that a mesh axis runs over, the one named last changes fastest.
Arguments:
- features: bfloat16 [32768, 768], P('dp'), may hold values from -6 to 6
- pos_conv: bfloat16 [32768, 768], P('dp'), may hold values from -3 to 3
- segment_ids: int32 [32, 1024], P('dp'), may hold values from 0 to 3, never falling along the last dimension, each value on 1 to 512 neighbouring positions
- frame_valid: int32 [32, 1024], P('dp'), may hold values 0 or 1
- cotangent: bfloat16 [32768, 768], P('dp'), may hold values from -6 to 6
- qkv_weight: float32 [768, 2304], P('dp'), may hold values from -0.21875 to 0.21875
- proj_weight: float32 [768, 768], P('dp'), may hold values from -1.75 to 1.75
- expand_weight: float32 [768, 3072], P('dp'), may hold values from -0.21875 to 0.21875
- reduce_weight: float32 [3072, 768], P('dp'), may hold values from -0.109375 to 0.109375
- norm_gains: float32 [2, 768], P(None, 'dp'), may hold values from 0.5 to 1.5
- bias_vector: float32 [7680], P('dp'), may hold values from -1.5 to 1.5
- qkv_moment: float32 [768, 2304], P('dp'), may hold values from -1086.116 to 1086.116
- proj_moment: float32 [768, 768], P('dp'), may hold values from -108.6116 to 108.6116
- expand_moment: float32 [768, 3072], P('dp'), may hold values from -325.8348 to 325.8348
- reduce_moment: float32 [3072, 768], P('dp'), may hold values from -651.6696 to 651.6696
- gains_moment: float32 [2, 768], P(None, 'dp'), may hold values from -1086.116 to 1086.116
- bias_moment: float32 [7680], P('dp'), may hold values from -1086.116 to 1086.116
- qkv_average: float32 [768, 2304], P('dp'), may hold values from -0.21875 to 0.21875
- proj_average: float32 [768, 768], P('dp'), may hold values from -1.75 to 1.75
- expand_average: float32 [768, 3072], P('dp'), may hold values from -0.21875 to 0.21875
- reduce_average: float32 [3072, 768], P('dp'), may hold values from -0.109375 to 0.109375
- gains_average: float32 [2, 768], P(None, 'dp'), may hold values from 0.5 to 1.5
- bias_average: float32 [7680], P('dp'), may hold values from -1.5 to 1.5
Outputs:
- layer_out: bfloat16 [32768, 768], P('dp')
- grad_input: bfloat16 [32768, 768], P('dp')
- qkv_grad: float32 [768, 2304], P('dp')
- proj_grad: float32 [768, 768], P('dp')
- expand_grad: float32 [768, 3072], P('dp')
- reduce_grad: float32 [3072, 768], P('dp')
- gains_grad: float32 [2, 768], P(None, 'dp')
- bias_grad: float32 [7680], P('dp')
- qkv_master: float32 [768, 2304], P('dp')
- proj_master: float32 [768, 768], P('dp')
- expand_master: float32 [768, 3072], P('dp')
- reduce_master: float32 [3072, 768], P('dp')
- gains_master: float32 [2, 768], P(None, 'dp')
- bias_master: float32 [7680], P('dp')
- qkv_velocity: float32 [768, 2304], P('dp')
- proj_velocity: float32 [768, 768], P('dp')
- expand_velocity: float32 [768, 3072], P('dp')
- reduce_velocity: float32 [3072, 768], P('dp')
- gains_velocity: float32 [2, 768], P(None, 'dp')
- bias_velocity: float32 [7680], P('dp')
- qkv_smooth: float32 [768, 2304], P('dp')
- proj_smooth: float32 [768, 768], P('dp')
- expand_smooth: float32 [768, 3072], P('dp')
- reduce_smooth: float32 [3072, 768], P('dp')
- gains_smooth: float32 [2, 768], P(None, 'dp')
- bias_smooth: float32 [7680], P('dp')
Inputs may be any that keep to these rules, and one draw needn't show every extreme that they name: `segment_ids`: each row lists one device's utterances: numbers 0 to 3 in order, each a run of 1 to 512 frames, one of exactly 512. `frame_valid`: 1 marks a frame with audio.
All inputs are finite; a program needn't handle non-finite values. No bound on the sum of `frame_valid` on one device may be relied on, other than what follows from the above.
Results may differ from a plain program's by a relative error of at most 0.015.
The roundings to bfloat16 on the way count: a program that leaves them out, or rounds other values in their place, can miss the bound.
Values may be sent and summed in bfloat16 or wider, within the bound.
A program may use at most 320 MiB of HBM per device.

v0:
```python
import math
import jax
import jax.numpy as jnp
from jax import lax
from jax.sharding import PartitionSpec as P

D = 768
H = 12
HD = 64
FF = 3072
EPSILON = 1e-05
MASKED = -1000000000.0
rate_matrix = 0.04
rate_proj = 0.5
rate_small = 0.2


def layer_norm(residual, gain_row, offset):
    center = residual - jnp.mean(residual, axis=-1, keepdims=True)
    spread = jnp.mean(center * center, axis=-1, keepdims=True)
    return center * lax.rsqrt(spread + EPSILON) * gain_row + offset


def gelu_exact(argument):
    return 0.5 * argument * (1.0 + jax.scipy.special.erf(argument * 0.7071067811865476))


def masked_scores(queries, key_heads, segments, present, first_row, block_rows):
    query_part = queries[first_row : first_row + block_rows]
    scores = (
        jnp.einsum("qhe,khe->hqk", query_part, key_heads, preferred_element_type=jnp.float32)
        * 0.125
    )
    column = jnp.arange(key_heads.shape[0])
    row_ids = column[first_row : first_row + block_rows]
    allowed = (segments[first_row : first_row + block_rows, None] == segments[None, :]) & (
        (present[None, :] > 0) | (row_ids[:, None] == column[None, :])
    )
    return (jnp.where(allowed[None], scores, MASKED), query_part)


def nesterov(master, gradient, moment, average, step_rate):
    velocity = 0.5 * moment + gradient
    renewed = master - step_rate * (gradient + 0.5 * velocity)
    smooth = 0.5 * average + 0.5 * renewed
    return (renewed, velocity, smooth)


def local(
    features,
    pos_conv,
    segment_ids,
    frame_valid,
    cotangent,
    qkv_weight,
    proj_weight,
    expand_weight,
    reduce_weight,
    norm_gains,
    bias_vector,
    qkv_moment,
    proj_moment,
    expand_moment,
    reduce_moment,
    gains_moment,
    bias_moment,
    qkv_average,
    proj_average,
    expand_average,
    reduce_average,
    gains_average,
    bias_average,
):
    row_count = features.shape[0]
    block_rows = min(512, row_count)
    segments = segment_ids[0]
    present = frame_valid[0]
    valid_col = present.astype(jnp.float32)[:, None]
    qkv_full, proj_full, expand_full, reduce_full, gains_low, bias_low = (
        lax.all_gather(qkv_weight.astype(jnp.bfloat16), "dp", axis=0, tiled=True),
        lax.all_gather(proj_weight.astype(jnp.bfloat16), "dp", axis=0, tiled=True),
        lax.all_gather(expand_weight.astype(jnp.bfloat16), "dp", axis=0, tiled=True),
        lax.all_gather(reduce_weight.astype(jnp.bfloat16), "dp", axis=0, tiled=True),
        lax.all_gather(norm_gains.astype(jnp.bfloat16), "dp", axis=1, tiled=True),
        lax.all_gather(bias_vector.astype(jnp.bfloat16), "dp", axis=0, tiled=True),
    )
    gains_full = gains_low.astype(jnp.float32)
    bias_full = bias_low.astype(jnp.float32)
    bias_query = bias_full[0:D]
    bias_value = bias_full[D : 2 * D]
    bias_proj = bias_full[2 * D : 3 * D]
    bias_expand = bias_full[3 * D : 3 * D + FF]
    bias_reduce = bias_full[3 * D + FF : 4 * D + FF]
    offset_first = bias_full[4 * D + FF : 5 * D + FF]
    offset_second = bias_full[5 * D + FF : 6 * D + FF]
    entry_sum = (features.astype(jnp.float32) + pos_conv.astype(jnp.float32)) * valid_col
    entry_low = entry_sum.astype(jnp.bfloat16)
    qkv_bias = jnp.concatenate([bias_query, jnp.zeros((D,), jnp.float32), bias_value])
    qkv_rows = (jnp.dot(entry_low, qkv_full, preferred_element_type=jnp.float32) + qkv_bias).astype(
        jnp.bfloat16
    )
    shaped = qkv_rows.reshape(row_count, 3, H, HD)
    queries = shaped[:, 0]
    key_heads = shaped[:, 1]
    values = shaped[:, 2]
    pieces = []
    log_totals = []
    for first_row in range(0, row_count, block_rows):
        scores, query_part = masked_scores(
            queries, key_heads, segments, present, first_row, block_rows
        )
        maximum = jnp.max(scores, axis=-1, keepdims=True)
        exponent = jnp.exp(scores - maximum)
        row_total = jnp.sum(exponent, axis=-1, keepdims=True)
        weights_now = (exponent / row_total).astype(jnp.bfloat16)
        pieces.append(
            jnp.einsum("hqk,khe->qhe", weights_now, values, preferred_element_type=jnp.float32)
        )
        log_totals.append(maximum + jnp.log(row_total))
    context = jnp.concatenate(pieces, axis=0).reshape(row_count, D).astype(jnp.bfloat16)
    attended = jnp.dot(context, proj_full, preferred_element_type=jnp.float32) + bias_proj
    normed, first_norm_back = jax.vjp(layer_norm, entry_sum + attended, gains_full[0], offset_first)
    normed_low = normed.astype(jnp.bfloat16)
    pre_act = jnp.dot(normed_low, expand_full, preferred_element_type=jnp.float32) + bias_expand
    activated, gelu_back = jax.vjp(gelu_exact, pre_act)
    act_low = activated.astype(jnp.bfloat16)
    ffn_out = jnp.dot(act_low, reduce_full, preferred_element_type=jnp.float32) + bias_reduce
    layer_float, second_norm_back = jax.vjp(
        layer_norm, normed + ffn_out, gains_full[1], offset_second
    )
    layer_out = layer_float.astype(jnp.bfloat16)
    qkv_back, proj_back, expand_back, reduce_back = (
        lax.all_gather(qkv_weight.astype(jnp.bfloat16), "dp", axis=0, tiled=True),
        lax.all_gather(proj_weight.astype(jnp.bfloat16), "dp", axis=0, tiled=True),
        lax.all_gather(expand_weight.astype(jnp.bfloat16), "dp", axis=0, tiled=True),
        lax.all_gather(reduce_weight.astype(jnp.bfloat16), "dp", axis=0, tiled=True),
    )
    grad_second, grad_gain_two, grad_offset_two = second_norm_back(cotangent.astype(jnp.float32))
    grad_ffn = grad_second.astype(jnp.bfloat16)
    grad_bias_reduce = jnp.sum(grad_ffn, axis=0, dtype=jnp.float32)
    grad_reduce = jnp.einsum("tf,td->fd", act_low, grad_ffn, preferred_element_type=jnp.float32)
    grad_hidden = jnp.einsum("td,fd->tf", grad_ffn, reduce_back, preferred_element_type=jnp.float32)
    (grad_pre_float,) = gelu_back(grad_hidden)
    grad_pre = grad_pre_float.astype(jnp.bfloat16)
    grad_bias_expand = jnp.sum(grad_pre, axis=0, dtype=jnp.float32)
    grad_expand = jnp.einsum("td,tf->df", normed_low, grad_pre, preferred_element_type=jnp.float32)
    grad_normed = grad_second + jnp.einsum(
        "tf,df->td", grad_pre, expand_back, preferred_element_type=jnp.float32
    )
    grad_first, grad_gain_one, grad_offset_one = first_norm_back(grad_normed)
    grad_branch = grad_first.astype(jnp.bfloat16)
    grad_bias_proj = jnp.sum(grad_branch, axis=0, dtype=jnp.float32)
    grad_proj = jnp.einsum("td,te->de", context, grad_branch, preferred_element_type=jnp.float32)
    grad_context = jnp.einsum(
        "te,de->td", grad_branch, proj_back, preferred_element_type=jnp.float32
    )
    grad_context = grad_context.astype(jnp.bfloat16).reshape(row_count, H, HD)
    query_grads = []
    key_grad = jnp.zeros((row_count, H, HD), jnp.float32)
    value_grad = jnp.zeros((row_count, H, HD), jnp.float32)
    for block_index, first_row in enumerate(range(0, row_count, block_rows)):
        scores, query_part = masked_scores(
            queries, key_heads, segments, present, first_row, block_rows
        )
        prob_block = jnp.exp(scores - log_totals[block_index])
        context_part = grad_context[first_row : first_row + block_rows]
        prob_grad = jnp.einsum(
            "qhe,khe->hqk", context_part, values, preferred_element_type=jnp.float32
        )
        row_dot = jnp.sum(prob_block * prob_grad, axis=-1, keepdims=True)
        score_grad = (prob_block * (prob_grad - row_dot)).astype(jnp.bfloat16)
        query_grads.append(
            0.125
            * jnp.einsum("hqk,khe->qhe", score_grad, key_heads, preferred_element_type=jnp.float32)
        )
        key_grad = key_grad + 0.125 * jnp.einsum(
            "hqk,qhe->khe", score_grad, query_part, preferred_element_type=jnp.float32
        )
        value_grad = value_grad + jnp.einsum(
            "hqk,qhe->khe",
            prob_block.astype(jnp.bfloat16),
            context_part,
            preferred_element_type=jnp.float32,
        )
    grad_qkv_low = jnp.stack([jnp.concatenate(query_grads, axis=0), key_grad, value_grad], axis=1)
    grad_qkv_low = grad_qkv_low.reshape(row_count, 3 * D).astype(jnp.bfloat16)
    grad_bias_query = jnp.sum(grad_qkv_low[:, 0:D], axis=0, dtype=jnp.float32)
    grad_bias_value = jnp.sum(grad_qkv_low[:, 2 * D : 3 * D], axis=0, dtype=jnp.float32)
    grad_qkv = jnp.einsum("td,te->de", entry_low, grad_qkv_low, preferred_element_type=jnp.float32)
    grad_entry = grad_first + jnp.einsum(
        "te,de->td", grad_qkv_low, qkv_back, preferred_element_type=jnp.float32
    )
    grad_input = (grad_entry * valid_col).astype(jnp.bfloat16)
    grad_gains = jnp.stack([grad_gain_one, grad_gain_two], axis=0)
    grad_bias = jnp.concatenate(
        [
            grad_bias_query,
            grad_bias_value,
            grad_bias_proj,
            grad_bias_expand,
            grad_bias_reduce,
            grad_offset_one,
            grad_offset_two,
        ]
    )
    qkv_grad, proj_grad, expand_grad, reduce_grad, gains_grad, bias_grad = (
        lax.psum_scatter(grad_qkv, "dp", scatter_dimension=0, tiled=True),
        lax.psum_scatter(grad_proj, "dp", scatter_dimension=0, tiled=True),
        lax.psum_scatter(grad_expand, "dp", scatter_dimension=0, tiled=True),
        lax.psum_scatter(grad_reduce, "dp", scatter_dimension=0, tiled=True),
        lax.psum_scatter(grad_gains, "dp", scatter_dimension=1, tiled=True),
        lax.psum_scatter(grad_bias, "dp", scatter_dimension=0, tiled=True),
    )
    frame_total = lax.axis_size("dp") * row_count
    matrix_rate = rate_matrix / math.sqrt(frame_total)
    proj_step = rate_proj / math.sqrt(frame_total)
    small_step = rate_small / math.sqrt(frame_total)
    qkv_new = nesterov(qkv_weight, qkv_grad, qkv_moment, qkv_average, matrix_rate)
    proj_new = nesterov(proj_weight, proj_grad, proj_moment, proj_average, proj_step)
    expand_new = nesterov(expand_weight, expand_grad, expand_moment, expand_average, matrix_rate)
    reduce_new = nesterov(reduce_weight, reduce_grad, reduce_moment, reduce_average, matrix_rate)
    gains_new = nesterov(norm_gains, gains_grad, gains_moment, gains_average, small_step)
    bias_new = nesterov(bias_vector, bias_grad, bias_moment, bias_average, small_step)
    return (
        layer_out,
        grad_input,
        qkv_grad,
        proj_grad,
        expand_grad,
        reduce_grad,
        gains_grad,
        bias_grad,
        qkv_new[0],
        proj_new[0],
        expand_new[0],
        reduce_new[0],
        gains_new[0],
        bias_new[0],
        qkv_new[1],
        proj_new[1],
        expand_new[1],
        reduce_new[1],
        gains_new[1],
        bias_new[1],
        qkv_new[2],
        proj_new[2],
        expand_new[2],
        reduce_new[2],
        gains_new[2],
        bias_new[2],
    )


def solution(mesh):
    in_specs = (
        P("dp", None),
        P("dp", None),
        P("dp", None),
        P("dp", None),
        P("dp", None),
        P("dp", None),
        P("dp", None),
        P("dp", None),
        P("dp", None),
        P(None, "dp"),
        P("dp"),
        P("dp", None),
        P("dp", None),
        P("dp", None),
        P("dp", None),
        P(None, "dp"),
        P("dp"),
        P("dp", None),
        P("dp", None),
        P("dp", None),
        P("dp", None),
        P(None, "dp"),
        P("dp"),
    )
    out_specs = (
        P("dp", None),
        P("dp", None),
        P("dp", None),
        P("dp", None),
        P("dp", None),
        P("dp", None),
        P(None, "dp"),
        P("dp"),
        P("dp", None),
        P("dp", None),
        P("dp", None),
        P("dp", None),
        P(None, "dp"),
        P("dp"),
        P("dp", None),
        P("dp", None),
        P("dp", None),
        P("dp", None),
        P(None, "dp"),
        P("dp"),
        P("dp", None),
        P("dp", None),
        P("dp", None),
        P("dp", None),
        P(None, "dp"),
        P("dp"),
    )
    return jax.shard_map(local, mesh=mesh, in_specs=in_specs, out_specs=out_specs, check_vma=False)
```

profile of v0, /device:TPU:0, one launch (start us, length us, event | category | flops | bytes accessed | tf_op | source)
XLA Modules:
  0.0 941.1 jit_solution(3668679954728577496)
XLA Ops:
  16.4 42.3 %all-reduce = bf16[7680]{0:T(1024)(128)(2,1)S(1)} all-reduce(bf16[7680]{0:T(1024)(128)(2,1)S(1)} %dynamic-update-slice), channel_id=1, replica_groups=mesh['dp'=32] {'dp'}, use_global_device_ids=true, to_apply=%add | all-reduce | flops 7680 | bytes 30720
  61.3 40.0 %all-gather = bf16[32,24,2]{1,2,0:T(2,128)(2,1)S(1)} all-gather(bf16[1,24,2]{1,2,0:T(2,128)(2,1)S(1)} %convert_bitcast_fusion), channel_id=1, replica_groups=mesh['dp'=32] {'dp'}, dimensions={0}, use_global_device_ids=true | all-gather | bytes 3168 | tf_op jit(solution)/shard_map/all_gather | solution.py:84
  107.1 2.0 fusion.21
  109.1 9.3 add_convert_fusion.1
  118.4 6.7 copy.80
  125.1 14.5 %fusion.13 = (f32[12,512]{1,0:T(8,128)S(1)}, f32[12,512,1024]{2,1,0:T(8,128)}) fusion(pred[512,1024]{1,0:T(8,128)(4,1)} %get-tuple-element.180, bf16[1024,3,12,64]{0,3,2,1:T(8,128)(2,1)} %bitcast.96), kind=kOutput, calls=%fused_computation.28 | convolution fusion | flops 824174592 | bytes 28073984 | tf_op jit(solution)/shard_map/qhe,khe->hqk/dot_general | solution.py:31
  139.6 12.4 %fusion.1 = f32[12,512]{1,0:T(8,128)S(1)} fusion(f32[12,512]{1,0:T(8,128)S(1)} %get-tuple-element.185, f32[12,512,1024]{2,1,0:T(8,128)} %get-tuple-element.186, pred[512,1024]{1,0:T(8,128)(4,1)} %get-tuple-element.180), kind=kLoop, calls=%fused_computation.13 | loop fusion | flops 25159680 | bytes 25739264 | tf_op jit(solution)/shard_map/reduce_sum | solution.py:114
  152.0 3.6 copy-done.1
  155.6 10.1 %fusion.35 = bf16[512,12,64]{0,2,1:T(8,128)(2,1)} fusion(f32[12,512]{1,0:T(8,128)S(1)} %fusion.1, f32[12,512]{1,0:T(8,128)S(1)} %get-tuple-element.185, f32[12,512,1024]{2,1,0:T(8,128)S(1)} %copy-done.1, pred[512,1024]{1,0:T(8,128)(4,1)} %get-tuple-element.180, bf16[1024,3,12,64]{0,3,2,1:T(8,128)(2,1)S(1)} %bitcast.101), kind=kOutput, calls=%fused_computation.80 | convolution fusion | flops 837156864 | bytes 28114944 | tf_op jit(solution)/shard_map/hqk,khe->qhe/dot_general | solution.py:117
  165.7 10.9 %fusion.12 = (f32[12,512]{1,0:T(8,128)S(1)}, f32[12,512,1024]{2,1,0:T(8,128)}) fusion(pred[512,1024]{1,0:T(8,128)(4,1)S(1)} %get-tuple-element.179, bf16[1024,3,12,64]{0,3,2,1:T(8,128)(2,1)S(1)} %bitcast.102), kind=kOutput, calls=%fused_computation.27 | convolution fusion | flops 824174592 | bytes 28073984 | tf_op jit(solution)/shard_map/qhe,khe->hqk/dot_general | solution.py:31
  176.6 13.5 %fusion = f32[12,512]{1,0:T(8,128)} fusion(f32[12,512]{1,0:T(8,128)S(1)} %get-tuple-element.187, f32[12,512,1024]{2,1,0:T(8,128)} %get-tuple-element.188, pred[512,1024]{1,0:T(8,128)(4,1)S(1)} %get-tuple-element.179), kind=kLoop, calls=%fused_computation.12 | loop fusion | flops 25159680 | bytes 25739264 | tf_op jit(solution)/shard_map/reduce_sum | solution.py:114
  190.1 2.7 copy-done
  192.8 9.7 %fusion.34 = bf16[512,12,64]{0,2,1:T(8,128)(2,1)} fusion(f32[12,512]{1,0:T(8,128)} %fusion, f32[12,512]{1,0:T(8,128)S(1)} %get-tuple-element.187, f32[12,512,1024]{2,1,0:T(8,128)S(1)} %copy-done, pred[512,1024]{1,0:T(8,128)(4,1)S(1)} %get-tuple-element.179, bf16[1024,3,12,64]{0,3,2,1:T(8,128)(2,1)S(1)} %bitcast.103), kind=kOutput, calls=%fused_computation.79 | convolution fusion | flops 837156864 | bytes 28106752 | tf_op jit(solution)/shard_map/hqk,khe->qhe/dot_general | solution.py:117
  202.5 2.7 pad_maximum_fusion.1
  205.2 4.6 fusion.63
  210.7 12.9 %multiply_convert_fusion.2 = (bf16[1024,3072]{1,0:T(8,128)(2,1)}, f32[1024,3072]{1,0:T(8,128)}) fusion(f32[3072]{0:T(1024)S(1)} %copy-done.47, bf16[768,3072]{1,0:T(8,128)(2,1)} %all-gather.10.cloned.1.call-done, f32[1024,768]{0,1:T(8,128)S(1)} %get-tuple-element.190, f32[768]{0:T(1024)S(1)} %copy-done.48, f32[768]{0:T(1024)S(1)} %copy-done.39, ...), kind=kOutput, calls=%fused_computation.22 | convolution fusion | flops 4854644736 | bytes 26765312 | tf_op jit(solution)/shard_map/dot_general | solution.py:124
  223.6 39.0 %all-gather.12.cloned.1.call-done = bf16[3072,768]{1,0:T(8,128)(2,1)} async-done(((bf16[96,768]{1,0:T(8,128)(2,1)}), bf16[3072,768]{1,0:T(8,128)(2,1)}) %all-gather.12.cloned.1.call-update) | async-done | bytes 4718608 | tf_op jit(solution)/shard_map/all_gather | solution.py:83
  262.6 9.1 fusion.64
  273.4 2.2 fusion.17
  275.6 3.5 convert_reduce_fusion.2
  279.2 15.4 %convert_reduce_fusion = (f32[3072]{0:T(1024)}, bf16[1024,3072]{1,0:T(8,128)(2,1)S(1)}) fusion(bf16[1024,768]{0,1:T(8,128)(2,1)S(1)} %get-tuple-element.165, bf16[3072,768]{1,0:T(8,128)(2,1)S(1)} %bitcast.128, f32[1024,3072]{1,0:T(8,128)} %get-tuple-element.192, f32[3072]{0:T(1024)S(1)} %copy-done.47), kind=kOutput, calls=%fused_computation.18 | convolution fusion | flops 4882166784 | bytes 25190400 | tf_op jit(solution)/shard_map/td,fd->tf/dot_general | solution.py:142
  294.6 7.1 multiply_reduce_fusion.2
  305.1 2.8 fusion.65
  310.4 13.6 %fusion.4 = f32[12,64,1024]{2,1,0:T(8,128)} fusion(bf16[512,12,64]{0,2,1:T(8,128)(2,1)S(1)} %bitcast.113, f32[12,512]{1,0:T(8,128)S(1)} %log_add_fusion, f32[12,512,1024]{2,1,0:T(8,128)} %get-tuple-element.186, pred[512,1024]{1,0:T(8,128)(4,1)S(1)} %copy-done.8), kind=kOutput, calls=%fused_computation.16 | convolution fusion | flops 830472192 | bytes 29646848 | tf_op jit(solution)/shard_map/hqk,qhe->khe/dot_general | solution.py:179
  324.0 20.3 %multiply_reduce_fusion = (f32[12,512]{1,0:T(8,128)S(1)}, f32[12,512,1024]{2,1,0:T(8,128)}) fusion(f32[12,512]{1,0:T(8,128)S(1)} %log_add_fusion, f32[12,512,1024]{2,1,0:T(8,128)} %get-tuple-element.186, pred[512,1024]{1,0:T(8,128)(4,1)S(1)} %copy-done.8, bf16[512,12,64]{0,2,1:T(8,128)(2,1)S(1)} %bitcast.114, bf16[1024,3,12,64]{0,3,2,1:T(8,128)(2,1)} %bitcast.97), kind=kOutput, calls=%fused_computation.1 | convolution fusion | flops 836757504 | bytes 53264384 | tf_op jit(solution)/shard_map/qhe,khe->hqk/dot_general | solution.py:167
  344.2 20.3 %multiply_reduce_fusion.1 = (f32[12,512]{1,0:T(8,128)S(1)}, f32[12,512,1024]{2,1,0:T(8,128)}) fusion(f32[12,512]{1,0:T(8,128)S(1)} %log_add_fusion.1, f32[12,512,1024]{2,1,0:T(8,128)} %get-tuple-element.188, pred[512,1024]{1,0:T(8,128)(4,1)S(1)} %copy-done.6, bf16[512,12,64]{0,2,1:T(8,128)(2,1)S(1)} %bitcast.111, bf16[1024,3,12,64]{0,3,2,1:T(8,128)(2,1)} %bitcast.98), kind=kOutput, calls=%fused_computation.4 | convolution fusion | flops 836757504 | bytes 53264384 | tf_op jit(solution)/shard_map/qhe,khe->hqk/dot_general | solution.py:167
  364.6 42.7 %multiply_convert_fusion = (bf16[12,512,1024]{2,1,0:T(8,128)(2,1)}, bf16[12,512,1024]{2,1,0:T(8,128)(2,1)}) fusion(f32[12,512,1024]{2,1,0:T(8,128)} %get-tuple-element.199, f32[12,512]{1,0:T(8,128)S(1)} %get-tuple-element.198, f32[12,512]{1,0:T(8,128)S(1)} %log_add_fusion, f32[12,512,1024]{2,1,0:T(8,128)} %get-tuple-element.186, ...), kind=kLoop, calls=%fused_computation | loop fusion | flops 75497472 | bytes 126976000 | tf_op jit(solution)/shard_map/convert_element_type | solution.py:171
  407.3 9.5 %fusion.32 = bf16[512,12,64]{0,2,1:T(8,128)(2,1)} fusion(bf16[12,512,1024]{2,1,0:T(8,128)(2,1)} %get-tuple-element.203, bf16[1024,3,12,64]{0,3,2,1:T(8,128)(2,1)S(1)} %bitcast.106), kind=kOutput, calls=%fused_computation.77 | convolution fusion | flops 806092800 | bytes 14942208 | tf_op jit(solution)/shard_map/hqk,khe->qhe/dot_general | solution.py:174
  416.8 8.6 fusion.40
  425.5 9.2 fusion.33
  434.7 7.5 fusion.29
  442.5 12.4 %fusion.26 = bf16[1024,1,12,64]{0,3,2,1:T(8,128)(2,1)S(1)} fusion(f32[12,64,1024]{2,1,0:T(8,128)S(1)} %copy-done.62, bf16[512,12,64]{0,2,1:T(8,128)(2,1)S(1)} %bitcast.112, f32[12,512]{1,0:T(8,128)S(1)} %log_add_fusion.1, f32[12,512,1024]{2,1,0:T(8,128)} %get-tuple-element.188, pred[512,1024]{1,0:T(8,128)(4,1)S(1)} %copy-done.7), kind=kOutput, calls=%fused_computation.73 | convolution fusion | flops 832045056 | bytes 31219712 | tf_op jit(solution)/shard_map/hqk,qhe->khe/dot_general | solution.py:179
  455.5 2.2 copy-done.9
  457.8 6.0 fusion.41
  463.8 1.8 copy-done.11
  465.6 10.5 %fusion.54 = f32[768,3072]{1,0:T(8,128)} fusion(bf16[1024,3072]{1,0:T(8,128)(2,1)} %copy-done.63, f32[1024,768]{0,1:T(8,128)S(1)} %copy-done.11, f32[768]{0:T(1024)S(1)} %copy-done.49, f32[768]{0:T(1024)S(1)} %copy-done.39, f32[1024]{0:T(1024)S(1)} %fusion.44, f32[1024]{0:T(1024)S(1)} %broadcast_multiply_fusion.1), kind=kOutput, calls=%fused_computation.141 | convolution fusion | flops 4835770368 | bytes 18888704 | tf_op jit(solution)/shard_map/td,tf->df/dot_general | solution.py:146
  477.5 10.5 %fusion.66 = f32[3072,768]{1,0:T(8,128)} fusion(bf16[1024,3072]{1,0:T(8,128)(2,1)} %get-tuple-element.191, bf16[1024,768]{0,1:T(8,128)(2,1)S(1)} %copy-done.24), kind=kOutput, calls=%fused_computation.151 | convolution fusion | flops 4831838208 | bytes 17301504 | tf_op jit(solution)/shard_map/tf,td->fd/dot_general | solution.py:141
  488.8 2.8 copy.86
  491.6 8.5 multiply_convert_fusion.3
  500.3 2.8 copy.87
  503.1 2.5 convert_reduce_fusion.4
  505.8 40.1 %all-reduce.3 = (f32[2,768]{1,0:T(2,128)S(1)}, f32[7680]{0:T(1024)S(1)}) all-reduce(f32[2,768]{1,0:T(2,128)S(1)} %pad_maximum_fusion.3, f32[7680]{0:T(1024)S(1)} %constant_dynamic-update-slice_fusion), channel_id=6, replica_groups=mesh['dp'=32] {'dp'}, use_global_device_ids=true, to_apply=%region_20.21.clone | all-reduce | flops 9216 | bytes 73728
  548.9 99.7 %reduce-scatter.6.cloned.1.call-done = f32[24,2304]{1,0:T(8,128)} async-done(((f32[768,2304]{1,0:T(8,128)}), f32[24,2304]{1,0:T(8,128)}) %reduce-scatter.6.cloned.1.call-update) | async-done | bytes 221200 | tf_op jit(solution)/shard_map/reduce_scatter | solution.py:207
  648.6 1.8 add_multiply_fusion.3
  650.4 139.4 %reduce-scatter.10.cloned.1.call-done = f32[24,3072]{1,0:T(8,128)} async-done(((f32[768,3072]{1,0:T(8,128)}), f32[24,3072]{1,0:T(8,128)}) %reduce-scatter.10.cloned.1.call-update) | async-done | bytes 294928 | tf_op jit(solution)/shard_map/reduce_scatter | solution.py:209
  789.8 1.9 add_multiply_fusion.2
  791.8 140.1 %reduce-scatter.12.cloned.1.call-done = f32[96,768]{1,0:T(8,128)} async-done(((f32[3072,768]{1,0:T(8,128)}), f32[96,768]{1,0:T(8,128)}) %reduce-scatter.12.cloned.1.call-update) | async-done | bytes 294928 | tf_op jit(solution)/shard_map/reduce_scatter | solution.py:210
  931.9 1.9 add_multiply_fusion.1
  (216 shorter events, 32.0 us)
Async XLA Ops:
  7.2 94.9 %copy-start.17 = (bf16[1024,768]{1,0:T(8,128)(2,1)S(1)}, bf16[1024,768]{1,0:T(8,128)(2,1)}, u32[]{:S(2)}) copy-start(bf16[1024,768]{1,0:T(8,128)(2,1)} %param.27) | copy-start | bytes 4718596
  7.2 96.6 %copy-start.18 = (bf16[1024,768]{1,0:T(8,128)(2,1)S(1)}, bf16[1024,768]{1,0:T(8,128)(2,1)}, u32[]{:S(2)}) copy-start(bf16[1024,768]{1,0:T(8,128)(2,1)} %param.23) | copy-start | bytes 4718596
  7.2 101.9 %all-gather.6.cloned.1.call-start = ((), (), s32[]{:S(2)}) async-start(), calls=%async_computation.4 | async-start | bytes 3649536 | tf_op jit(solution)/shard_map/all_gather | solution.py:80
  9.0 196.1 %all-gather.8.cloned.1.call-start = ((), (), s32[]{:S(2)}) async-start(), calls=%async_computation.5 | async-start | bytes 1216512 | tf_op jit(solution)/shard_map/all_gather | solution.py:81
  10.6 200.0 %all-gather.10.cloned.1.call-start = ((), (), s32[]{:S(2)}) async-start(), calls=%async_computation.6 | async-start | bytes 4866048 | tf_op jit(solution)/shard_map/all_gather | solution.py:82
  12.3 250.3 %all-gather.12.cloned.1.call-start = ((), (), s32[]{:S(2)}) async-start(), calls=%async_computation.7 | async-start | bytes 4866048 | tf_op jit(solution)/shard_map/all_gather | solution.py:83
  14.1 533.3 %reduce-scatter.8.cloned.1.call-start = ((), (), s32[]{:S(2)}) async-start(), calls=%async_computation.9 | async-start | bytes 2433024 | tf_op jit(solution)/shard_map/reduce_scatter | solution.py:208
  15.5 189.7 %copy-start.52 = (f32[1,1024]{1,0:T(1,128)}, f32[1,1024]{1,0:T(1,128)S(1)}, u32[]{:S(2)}) copy-start(f32[1,1024]{1,0:T(1,128)S(1)} %convert_element_type.120) | copy-start | bytes 12292
  109.1 81.0 %copy-start.5 = (pred[512,1024]{1,0:T(8,128)(4,1)}, pred[512,1024]{1,0:T(8,128)(4,1)S(1)}, u32[]{:S(2)}) copy-start(pred[512,1024]{1,0:T(8,128)(4,1)S(1)} %get-tuple-element.179) | copy-start | bytes 1572868
  125.1 27.0 %copy-start.2 = (bf16[1024,2304]{0,1:T(8,128)(2,1)S(1)}, bf16[1024,2304]{0,1:T(8,128)(2,1)}, u32[]{:S(2)}) copy-start(bf16[1024,2304]{0,1:T(8,128)(2,1)} %copy.80) | copy-start | bytes 14155780
  139.6 16.0 %copy-start.1 = (f32[12,512,1024]{2,1,0:T(8,128)S(1)}, f32[12,512,1024]{2,1,0:T(8,128)}, u32[]{:S(2)}) copy-start(f32[12,512,1024]{2,1,0:T(8,128)} %get-tuple-element.186) | copy-start | bytes 75497472
  176.6 16.1 %copy-start = (f32[12,512,1024]{2,1,0:T(8,128)S(1)}, f32[12,512,1024]{2,1,0:T(8,128)}, u32[]{:S(2)}) copy-start(f32[12,512,1024]{2,1,0:T(8,128)} %get-tuple-element.188) | copy-start | bytes 75497472
  209.8 91.8 %copy-start.10 = (f32[1024,768]{0,1:T(8,128)}, f32[1024,768]{0,1:T(8,128)S(1)}, u32[]{:S(2)}) copy-start(f32[1024,768]{0,1:T(8,128)S(1)} %get-tuple-element.190) | copy-start | bytes 9437188
  210.7 51.9 %copy-start.50 = (f32[768]{0:T(1024)S(1)}, f32[768]{0:T(1024)}, u32[]{:S(2)}) copy-start(f32[768]{0:T(1024)} %get-tuple-element.174) | copy-start | bytes 9220
  262.6 9.1 copy-start.4
  262.6 9.1 copy-start.38
  275.6 19.0 %slice-start.2 = ((s8[4718592]{0:T(1024)(128)(4,1)}), s8[4194304]{0:T(1024)(128)(4,1)S(1)}, s32[]{:S(2)}) async-start(s8[4718592]{0:T(1024)(128)(4,1)} %bitcast.125), calls=%async_computation.14 | async-start | bytes 8388608
  279.2 15.4 %copy-start.23 = (bf16[1024,768]{0,1:T(8,128)(2,1)}, bf16[1024,768]{0,1:T(8,128)(2,1)S(1)}, u32[]{:S(2)}) copy-start(bf16[1024,768]{0,1:T(8,128)(2,1)S(1)} %get-tuple-element.165) | copy-start | bytes 4718596
  279.2 15.4 %slice-start.3 = ((s8[4718592]{0:T(1024)(128)(4,1)}), s8[524288]{0:T(1024)(128)(4,1)S(1)}, s32[]{:S(2)}) async-start(s8[4718592]{0:T(1024)(128)(4,1)} %bitcast.125), calls=%async_computation.15 | async-start | bytes 1048576
  309.4 34.8 %copy-start.15 = (bf16[512,768]{0,1:T(8,128)(2,1)}, bf16[512,768]{0,1:T(8,128)(2,1)S(1)}, u32[]{:S(2)}) copy-start(bf16[512,768]{0,1:T(8,128)(2,1)S(1)} %get-tuple-element.171) | copy-start | bytes 2359300
  324.0 20.3 %copy-start.6 = (pred[512,1024]{1,0:T(8,128)(4,1)S(1)}, pred[512,1024]{1,0:T(8,128)(4,1)}, u32[]{:S(2)}) copy-start(pred[512,1024]{1,0:T(8,128)(4,1)} %copy-done.5) | copy-start | bytes 1572868
  344.2 63.1 %slice-start = ((s8[4718592]{0:T(1024)(128)(4,1)}), s8[524288]{0:T(1024)(128)(4,1)S(1)}, s32[]{:S(2)}) async-start(s8[4718592]{0:T(1024)(128)(4,1)} %bitcast.104), calls=%async_computation.12 | async-start | bytes 1048576
  364.6 42.7 %slice-start.1 = ((s8[4718592]{0:T(1024)(128)(4,1)}), s8[4194304]{0:T(1024)(128)(4,1)S(1)}, s32[]{:S(2)}) async-start(s8[4718592]{0:T(1024)(128)(4,1)} %bitcast.104), calls=%async_computation.13 | async-start | bytes 8388608
  425.4 223.2 %reduce-scatter.6.cloned.1.call-start = ((), (), s32[]{:S(2)}) async-start(), calls=%async_computation.8 | async-start | bytes 7299072 | tf_op jit(solution)/shard_map/reduce_scatter | solution.py:207
  425.5 9.2 copy-start.3
  434.7 7.8 copy-start.7
  434.7 7.8 copy-start.16
  434.7 7.8 copy-start.62
  463.8 326.1 %reduce-scatter.10.cloned.1.call-start = ((), (), s32[]{:S(2)}) async-start(), calls=%async_computation.10 | async-start | bytes 9732096 | tf_op jit(solution)/shard_map/reduce_scatter | solution.py:209
  476.1 455.8 %reduce-scatter.12.cloned.1.call-start = ((), (), s32[]{:S(2)}) async-start(), calls=%async_computation.11 | async-start | bytes 9732096 | tf_op jit(solution)/shard_map/reduce_scatter | solution.py:210
  500.2 45.8 %copy-start.55 = (f32[2,24]{1,0:T(2,128)S(1)}, f32[2,24]{1,0:T(2,128)}, u32[]{:S(2)}) copy-start(f32[2,24]{1,0:T(2,128)} %param.32) | copy-start | bytes 580
  500.2 45.8 %copy-start.56 = (f32[2,24]{1,0:T(2,128)S(1)}, f32[2,24]{1,0:T(2,128)}, u32[]{:S(2)}) copy-start(f32[2,24]{1,0:T(2,128)} %param.44) | copy-start | bytes 580
  500.2 45.8 %copy-start.57 = (f32[2,24]{1,0:T(2,128)S(1)}, f32[2,24]{1,0:T(2,128)}, u32[]{:S(2)}) copy-start(f32[2,24]{1,0:T(2,128)} %param.38) | copy-start | bytes 580
  500.2 46.4 %copy-start.58 = (f32[240]{0:T(256)S(1)}, f32[240]{0:T(256)}, u32[]{:S(2)}) copy-start(f32[240]{0:T(256)} %param.33) | copy-start | bytes 2884
  500.2 46.4 %copy-start.59 = (f32[240]{0:T(256)S(1)}, f32[240]{0:T(256)}, u32[]{:S(2)}) copy-start(f32[240]{0:T(256)} %param.45) | copy-start | bytes 2884
  500.2 46.4 %copy-start.60 = (f32[240]{0:T(256)S(1)}, f32[240]{0:T(256)}, u32[]{:S(2)}) copy-start(f32[240]{0:T(256)} %param.39) | copy-start | bytes 2884
  500.2 47.1 %copy-start.28 = (f32[24,768]{1,0:T(8,128)S(1)}, f32[24,768]{1,0:T(8,128)}, u32[]{:S(2)}) copy-start(f32[24,768]{1,0:T(8,128)} %param.29) | copy-start | bytes 221188
  500.3 47.0 %copy-start.36 = (f32[24,768]{1,0:T(8,128)S(1)}, f32[24,768]{1,0:T(8,128)}, u32[]{:S(2)}) copy-start(f32[24,768]{1,0:T(8,128)} %param.41) | copy-start | bytes 221188
  500.3 47.0 %copy-start.37 = (f32[24,768]{1,0:T(8,128)S(1)}, f32[24,768]{1,0:T(8,128)}, u32[]{:S(2)}) copy-start(f32[24,768]{1,0:T(8,128)} %param.35) | copy-start | bytes 221188
  500.3 148.3 %copy-start.27 = (f32[24,2304]{1,0:T(8,128)S(1)}, f32[24,2304]{1,0:T(8,128)}, u32[]{:S(2)}) copy-start(f32[24,2304]{1,0:T(8,128)} %param.28) | copy-start | bytes 663556
  500.3 148.3 %copy-start.33 = (f32[24,2304]{1,0:T(8,128)S(1)}, f32[24,2304]{1,0:T(8,128)}, u32[]{:S(2)}) copy-start(f32[24,2304]{1,0:T(8,128)} %param.40) | copy-start | bytes 663556
  500.3 148.3 %copy-start.34 = (f32[24,2304]{1,0:T(8,128)S(1)}, f32[24,2304]{1,0:T(8,128)}, u32[]{:S(2)}) copy-start(f32[24,2304]{1,0:T(8,128)} %param.34) | copy-start | bytes 663556
  503.1 286.7 %copy-start.25 = (f32[24,3072]{1,0:T(8,128)S(1)}, f32[24,3072]{1,0:T(8,128)}, u32[]{:S(2)}) copy-start(f32[24,3072]{1,0:T(8,128)} %param.30) | copy-start | bytes 884740
  503.1 286.7 %copy-start.29 = (f32[24,3072]{1,0:T(8,128)S(1)}, f32[24,3072]{1,0:T(8,128)}, u32[]{:S(2)}) copy-start(f32[24,3072]{1,0:T(8,128)} %param.42) | copy-start | bytes 884740
  503.1 286.7 %copy-start.30 = (f32[24,3072]{1,0:T(8,128)S(1)}, f32[24,3072]{1,0:T(8,128)}, u32[]{:S(2)}) copy-start(f32[24,3072]{1,0:T(8,128)} %param.36) | copy-start | bytes 884740
  503.1 428.8 %copy-start.26 = (f32[96,768]{1,0:T(8,128)S(1)}, f32[96,768]{1,0:T(8,128)}, u32[]{:S(2)}) copy-start(f32[96,768]{1,0:T(8,128)} %param.31) | copy-start | bytes 884740
  503.1 428.8 %copy-start.31 = (f32[96,768]{1,0:T(8,128)S(1)}, f32[96,768]{1,0:T(8,128)}, u32[]{:S(2)}) copy-start(f32[96,768]{1,0:T(8,128)} %param.43) | copy-start | bytes 884740
  503.1 428.8 %copy-start.32 = (f32[96,768]{1,0:T(8,128)S(1)}, f32[96,768]{1,0:T(8,128)}, u32[]{:S(2)}) copy-start(f32[96,768]{1,0:T(8,128)} %param.37) | copy-start | bytes 884740
  (30 other events, 95.3 us)
Sparse Core Ops, SparseCore 0:
  11.5 62.8 all-gather.5
  77.9 52.8 all-gather.7
  134.2 62.5 all-gather.9
  200.2 62.3 all-gather.11
  425.5 97.9 reduce-scatter.7
  530.5 117.9 reduce-scatter.5
  655.1 134.7 reduce-scatter.9
  797.3 134.5 reduce-scatter.11
where the time goes:
time: 952 us; the launch traced here: 941 us
  waiting for transfers between devices  418 us (44%)
  matrix products  245 us (26%)
  blocking collectives  122 us (13%)
  other arithmetic  104 us (11%)
  local copies, waits for them, and re-layouts  35.9 us (4%)
  between operations  15.4 us (2%)
    reduce_scatter x1, waiting for transfers between devices, local(): lax.psum_scatter(grad_reduce, 'dp', scatter_dimension=0, tiled=True)  140 us
    reduce_scatter x1, waiting for transfers between devices, local(): lax.psum_scatter(grad_expand, 'dp', scatter_dimension=0, tiled=True)  139 us
    reduce_scatter x1, waiting for transfers between devices, local(): lax.psum_scatter(grad_qkv, 'dp', scatter_dimension=0, tiled=True)  99.7 us
    unnamed x2, blocking collectives  82.4 us
    convert_element_type x1, other arithmetic, local(): score_grad = (prob_block * (prob_grad - row_dot)).astype(jnp.bfloat16)  42.7 us
    dot_general x2, matrix products, local(): jnp.einsum('qhe,khe->hqk', context_part, values, preferred_element_type=j...  40.6 us
    all_gather x1, blocking collectives, local(): lax.all_gather(norm_gains.astype(jnp.bfloat16), 'dp', axis=1, tiled=True)  40 us
    all_gather x1, waiting for transfers between devices, local(): lax.all_gather(reduce_weight.astype(jnp.bfloat16), 'dp', axis=0, tiled=True)  39 us
  transfers between devices with their start and end apart: 8, of which 4 were waited for; matrix products, arithmetic and copies ran while one was open for 22% of the time, Pallas kernels for 0%

commit v1 on v0

--- a/solution.py
+++ b/solution.py
@@ -13,6 +13,18 @@
 rate_matrix = 0.04
 rate_proj = 0.5
 rate_small = 0.2
+
+
+def gather_by_bits(array, axis, dim):
+    ways, here, step = (lax.axis_size(axis), lax.axis_index(axis), array.shape[dim])
+    line, have = (array, 1)
+    while have < ways:
+        line = jnp.concatenate(
+            [line, lax.ppermute(line, axis, [(d, (d - have) % ways) for d in range(ways)])],
+            axis=dim,
+        )
+        have = 2 * have
+    return jnp.roll(line, here * step, axis=dim)
 
 
 def layer_norm(residual, gain_row, offset):
@@ -81,7 +93,7 @@
         lax.all_gather(proj_weight.astype(jnp.bfloat16), "dp", axis=0, tiled=True),
         lax.all_gather(expand_weight.astype(jnp.bfloat16), "dp", axis=0, tiled=True),
         lax.all_gather(reduce_weight.astype(jnp.bfloat16), "dp", axis=0, tiled=True),
-        lax.all_gather(norm_gains.astype(jnp.bfloat16), "dp", axis=1, tiled=True),
+        gather_by_bits(norm_gains.astype(jnp.bfloat16), "dp", 1),
         lax.all_gather(bias_vector.astype(jnp.bfloat16), "dp", axis=0, tiled=True),
     )
     gains_full = gains_low.astype(jnp.float32)

time: 952 us -> 945 us (level)
  blocking collectives: 122 us -> 80.6 us
  waiting for transfers between devices: 418 us -> 448 us
  starting transfers between devices: 0.33 us -> 11.7 us
    all_gather x1 -> x0, blocking collectives: 40 us -> none  [local(): lax.all_gather(norm_gains.astype(jnp.bfloat16), 'dp', axis=1, tiled=True)]
    all_gather x1, waiting for transfers between devices: 39 us -> 53 us  [local(): lax.all_gather(reduce_weight.astype(jnp.bfloat16), 'dp', axis=0, tiled=True)]
    ppermute x0 -> x5, starting transfers between devices: none -> 11.4 us  [gather_by_bits(): lax.ppermute(line, axis, [(d, (d - have) % ways) for d in range(ways)])]
    all_gather x1, waiting for transfers between devices: 0.02 us -> 11.4 us  [local(): lax.all_gather(expand_weight.astype(jnp.bfloat16), 'dp', axis=0, tiled=True)]
    unnamed x153 -> x147, local copies, waits for them, and re-layouts: 26.3 us -> 27.6 us
  transfers between devices with their start and end apart: 8 -> 13, of which waited for: 4 -> 7; matrix products, arithmetic and copies ran while one was open for 22% -> 22% of each run, Pallas kernels for 0% -> 0%
where the time goes in v1:
time: 945 us; the launch traced here: 941 us
  waiting for transfers between devices  448 us (47%)
  matrix products  244 us (26%)
  other arithmetic  104 us (11%)
  blocking collectives  80.6 us (9%)
  local copies, waits for them, and re-layouts  37.1 us (4%)
  between operations  15.2 us (2%)
  starting transfers between devices  11.7 us (1%)
    reduce_scatter x1, waiting for transfers between devices, local(): lax.psum_scatter(grad_reduce, 'dp', scatter_dimension=0, tiled=True)  140 us
    reduce_scatter x1, waiting for transfers between devices, local(): lax.psum_scatter(grad_expand, 'dp', scatter_dimension=0, tiled=True)  139 us
    reduce_scatter x1, waiting for transfers between devices, local(): lax.psum_scatter(grad_qkv, 'dp', scatter_dimension=0, tiled=True)  99.9 us
    unnamed x2, blocking collectives  80.6 us
    all_gather x1, waiting for transfers between devices, local(): lax.all_gather(reduce_weight.astype(jnp.bfloat16), 'dp', axis=0, tiled=True)  53 us
    convert_element_type x1, other arithmetic, local(): score_grad = (prob_block * (prob_grad - row_dot)).astype(jnp.bfloat16)  43 us
    dot_general x2, matrix products, local(): jnp.einsum('qhe,khe->hqk', context_part, values, preferred_element_type=j...  40.5 us
    unnamed x147, local copies, waits for them, and re-layouts  27.6 us
  transfers between devices with their start and end apart: 13, of which 7 were waited for; matrix products, arithmetic and copies ran while one was open for 22% of the time, Pallas kernels for 0%

profile of v1, /device:TPU:0, one launch (start us, length us, event | category | flops | bytes accessed | tf_op | source)
XLA Modules:
  0.0 941.2 jit_solution(9149370025845225686)
XLA Ops:
  13.0 6.4 collective-permute-start
  23.2 2.6 fusion.21
  26.7 2.8 collective-permute-done.1
  30.1 40.4 %all-reduce = bf16[7680]{0:T(1024)(128)(2,1)S(1)} all-reduce(bf16[7680]{0:T(1024)(128)(2,1)S(1)} %dynamic-update-slice), channel_id=1, replica_groups=mesh['dp'=32] {'dp'}, use_global_device_ids=true, to_apply=%add | all-reduce | flops 7680 | bytes 30720
  74.4 2.1 collective-permute-start.4
  79.5 2.8 copy.68
  84.7 9.1 add_convert_fusion.1
  93.8 6.7 copy.70
  100.5 14.5 %fusion.13 = (f32[12,512]{1,0:T(8,128)S(1)}, f32[12,512,1024]{2,1,0:T(8,128)}) fusion(pred[512,1024]{1,0:T(8,128)(4,1)} %get-tuple-element.154, bf16[1024,3,12,64]{0,3,2,1:T(8,128)(2,1)} %bitcast.89), kind=kOutput, calls=%fused_computation.28 | convolution fusion | flops 824174592 | bytes 28073984 | tf_op jit(solution)/shard_map/qhe,khe->hqk/dot_general | solution.py:43
  115.1 12.3 %fusion.1 = f32[12,512]{1,0:T(8,128)S(1)} fusion(f32[12,512]{1,0:T(8,128)S(1)} %get-tuple-element.159, f32[12,512,1024]{2,1,0:T(8,128)} %get-tuple-element.160, pred[512,1024]{1,0:T(8,128)(4,1)} %get-tuple-element.154), kind=kLoop, calls=%fused_computation.13 | loop fusion | flops 25159680 | bytes 25739264 | tf_op jit(solution)/shard_map/reduce_sum | solution.py:126
  127.4 3.8 copy-done.1
  131.2 10.0 %fusion.35 = bf16[512,12,64]{0,2,1:T(8,128)(2,1)} fusion(f32[12,512]{1,0:T(8,128)S(1)} %fusion.1, f32[12,512]{1,0:T(8,128)S(1)} %get-tuple-element.159, f32[12,512,1024]{2,1,0:T(8,128)S(1)} %copy-done.1, pred[512,1024]{1,0:T(8,128)(4,1)} %get-tuple-element.154, bf16[1024,3,12,64]{0,3,2,1:T(8,128)(2,1)S(1)} %bitcast.94), kind=kOutput, calls=%fused_computation.80 | convolution fusion | flops 837156864 | bytes 28114944 | tf_op jit(solution)/shard_map/hqk,khe->qhe/dot_general | solution.py:129
  141.2 11.0 %fusion.12 = (f32[12,512]{1,0:T(8,128)S(1)}, f32[12,512,1024]{2,1,0:T(8,128)}) fusion(pred[512,1024]{1,0:T(8,128)(4,1)S(1)} %get-tuple-element.153, bf16[1024,3,12,64]{0,3,2,1:T(8,128)(2,1)S(1)} %bitcast.95), kind=kOutput, calls=%fused_computation.27 | convolution fusion | flops 824174592 | bytes 28073984 | tf_op jit(solution)/shard_map/qhe,khe->hqk/dot_general | solution.py:43
  152.1 12.9 %fusion = f32[12,512]{1,0:T(8,128)} fusion(f32[12,512]{1,0:T(8,128)S(1)} %get-tuple-element.161, f32[12,512,1024]{2,1,0:T(8,128)} %get-tuple-element.162, pred[512,1024]{1,0:T(8,128)(4,1)S(1)} %get-tuple-element.153), kind=kLoop, calls=%fused_computation.12 | loop fusion | flops 25159680 | bytes 25739264 | tf_op jit(solution)/shard_map/reduce_sum | solution.py:126
  165.1 2.7 copy-done
  167.7 9.9 %fusion.34 = bf16[512,12,64]{0,2,1:T(8,128)(2,1)} fusion(f32[12,512]{1,0:T(8,128)} %fusion, f32[12,512]{1,0:T(8,128)S(1)} %get-tuple-element.161, f32[12,512,1024]{2,1,0:T(8,128)S(1)} %copy-done, pred[512,1024]{1,0:T(8,128)(4,1)S(1)} %get-tuple-element.153, bf16[1024,3,12,64]{0,3,2,1:T(8,128)(2,1)S(1)} %bitcast.96), kind=kOutput, calls=%fused_computation.79 | convolution fusion | flops 837156864 | bytes 28106752 | tf_op jit(solution)/shard_map/hqk,khe->qhe/dot_general | solution.py:129
  177.7 2.7 pad_maximum_fusion.1
  180.4 4.6 fusion.63
  185.7 11.4 %all-gather.9.cloned.1.call-done = bf16[768,3072]{1,0:T(8,128)(2,1)} async-done(((bf16[24,3072]{1,0:T(8,128)(2,1)}), bf16[768,3072]{1,0:T(8,128)(2,1)}) %all-gather.9.cloned.1.call-update) | async-done | bytes 4718608 | tf_op jit(solution)/shard_map/all_gather | solution.py:94
  197.1 12.7 %multiply_convert_fusion.2 = (bf16[1024,3072]{1,0:T(8,128)(2,1)}, f32[1024,3072]{1,0:T(8,128)}) fusion(f32[3072]{0:T(1024)S(1)} %copy-done.44, bf16[768,3072]{1,0:T(8,128)(2,1)} %all-gather.9.cloned.1.call-done, f32[1024,768]{0,1:T(8,128)S(1)} %get-tuple-element.164, f32[768]{0:T(1024)S(1)} %copy-done.45, f32[768]{0:T(1024)S(1)} %get-tuple-element.115, ...), kind=kOutput, calls=%fused_computation.22 | convolution fusion | flops 4854644736 | bytes 26765312 | tf_op jit(solution)/shard_map/dot_general | solution.py:136
  209.9 53.0 %all-gather.11.cloned.1.call-done = bf16[3072,768]{1,0:T(8,128)(2,1)} async-done(((bf16[96,768]{1,0:T(8,128)(2,1)}), bf16[3072,768]{1,0:T(8,128)(2,1)}) %all-gather.11.cloned.1.call-update) | async-done | bytes 4718608 | tf_op jit(solution)/shard_map/all_gather | solution.py:95
  262.9 9.0 fusion.64
  273.7 2.2 fusion.17
  275.9 3.5 convert_reduce_fusion.2
  279.4 15.4 %convert_reduce_fusion = (f32[3072]{0:T(1024)}, bf16[1024,3072]{1,0:T(8,128)(2,1)S(1)}) fusion(bf16[1024,768]{0,1:T(8,128)(2,1)S(1)} %get-tuple-element.139, bf16[3072,768]{1,0:T(8,128)(2,1)S(1)} %bitcast.120, f32[1024,3072]{1,0:T(8,128)} %get-tuple-element.166, f32[3072]{0:T(1024)S(1)} %copy-done.44), kind=kOutput, calls=%fused_computation.18 | convolution fusion | flops 4882166784 | bytes 25190400 | tf_op jit(solution)/shard_map/td,fd->tf/dot_general | solution.py:154
  294.8 7.1 multiply_reduce_fusion.2
  305.3 2.8 fusion.65
  310.7 13.4 %fusion.4 = f32[12,64,1024]{2,1,0:T(8,128)} fusion(bf16[512,12,64]{0,2,1:T(8,128)(2,1)S(1)} %bitcast.106, f32[12,512]{1,0:T(8,128)S(1)} %log_add_fusion, f32[12,512,1024]{2,1,0:T(8,128)} %get-tuple-element.160, pred[512,1024]{1,0:T(8,128)(4,1)S(1)} %copy-done.8), kind=kOutput, calls=%fused_computation.16 | convolution fusion | flops 830472192 | bytes 29646848 | tf_op jit(solution)/shard_map/hqk,qhe->khe/dot_general | solution.py:191
  324.0 20.2 %multiply_reduce_fusion = (f32[12,512]{1,0:T(8,128)S(1)}, f32[12,512,1024]{2,1,0:T(8,128)}) fusion(f32[12,512]{1,0:T(8,128)S(1)} %log_add_fusion, f32[12,512,1024]{2,1,0:T(8,128)} %get-tuple-element.160, pred[512,1024]{1,0:T(8,128)(4,1)S(1)} %copy-done.8, bf16[512,12,64]{0,2,1:T(8,128)(2,1)S(1)} %bitcast.107, bf16[1024,3,12,64]{0,3,2,1:T(8,128)(2,1)} %bitcast.90), kind=kOutput, calls=%fused_computation.1 | convolution fusion | flops 836757504 | bytes 53264384 | tf_op jit(solution)/shard_map/qhe,khe->hqk/dot_general | solution.py:179
  344.3 20.3 %multiply_reduce_fusion.1 = (f32[12,512]{1,0:T(8,128)S(1)}, f32[12,512,1024]{2,1,0:T(8,128)}) fusion(f32[12,512]{1,0:T(8,128)S(1)} %log_add_fusion.1, f32[12,512,1024]{2,1,0:T(8,128)} %get-tuple-element.162, pred[512,1024]{1,0:T(8,128)(4,1)S(1)} %copy-done.6, bf16[512,12,64]{0,2,1:T(8,128)(2,1)S(1)} %bitcast.104, bf16[1024,3,12,64]{0,3,2,1:T(8,128)(2,1)} %bitcast.91), kind=kOutput, calls=%fused_computation.4 | convolution fusion | flops 836757504 | bytes 53264384 | tf_op jit(solution)/shard_map/qhe,khe->hqk/dot_general | solution.py:179
  364.6 43.0 %multiply_convert_fusion = (bf16[12,512,1024]{2,1,0:T(8,128)(2,1)}, bf16[12,512,1024]{2,1,0:T(8,128)(2,1)}) fusion(f32[12,512,1024]{2,1,0:T(8,128)} %get-tuple-element.173, f32[12,512]{1,0:T(8,128)S(1)} %get-tuple-element.172, f32[12,512]{1,0:T(8,128)S(1)} %log_add_fusion, f32[12,512,1024]{2,1,0:T(8,128)} %get-tuple-element.160, ...), kind=kLoop, calls=%fused_computation | loop fusion | flops 75497472 | bytes 126976000 | tf_op jit(solution)/shard_map/convert_element_type | solution.py:183
  407.6 9.5 %fusion.32 = bf16[512,12,64]{0,2,1:T(8,128)(2,1)} fusion(bf16[12,512,1024]{2,1,0:T(8,128)(2,1)} %get-tuple-element.177, bf16[1024,3,12,64]{0,3,2,1:T(8,128)(2,1)S(1)} %bitcast.99), kind=kOutput, calls=%fused_computation.77 | convolution fusion | flops 806092800 | bytes 14942208 | tf_op jit(solution)/shard_map/hqk,khe->qhe/dot_general | solution.py:186
  417.1 8.6 fusion.40
  425.7 9.2 fusion.33
  434.9 7.5 fusion.29
  442.7 12.4 %fusion.26 = bf16[1024,1,12,64]{0,3,2,1:T(8,128)(2,1)S(1)} fusion(f32[12,64,1024]{2,1,0:T(8,128)S(1)} %copy-done.59, bf16[512,12,64]{0,2,1:T(8,128)(2,1)S(1)} %bitcast.105, f32[12,512]{1,0:T(8,128)S(1)} %log_add_fusion.1, f32[12,512,1024]{2,1,0:T(8,128)} %get-tuple-element.162, pred[512,1024]{1,0:T(8,128)(4,1)S(1)} %copy-done.7), kind=kOutput, calls=%fused_computation.73 | convolution fusion | flops 832045056 | bytes 31219712 | tf_op jit(solution)/shard_map/hqk,qhe->khe/dot_general | solution.py:191
  455.7 2.2 copy-done.9
  458.0 6.0 fusion.41
  465.8 10.5 %fusion.54 = f32[768,3072]{1,0:T(8,128)} fusion(bf16[1024,3072]{1,0:T(8,128)(2,1)} %copy-done.60, f32[1024,768]{0,1:T(8,128)S(1)} %copy-done.11, f32[768]{0:T(1024)S(1)} %copy-done.46, f32[768]{0:T(1024)S(1)} %get-tuple-element.115, f32[1024]{0:T(1024)S(1)} %fusion.44, f32[1024]{0:T(1024)S(1)} %broadcast_multiply_fusion.1), kind=kOutput, calls=%fused_computation.144 | convolution fusion | flops 4835770368 | bytes 18888704 | tf_op jit(solution)/shard_map/td,tf->df/dot_general | solution.py:158
  477.7 10.4 %fusion.66 = f32[3072,768]{1,0:T(8,128)} fusion(bf16[1024,3072]{1,0:T(8,128)(2,1)} %get-tuple-element.165, bf16[1024,768]{0,1:T(8,128)(2,1)S(1)} %copy-done.23), kind=kOutput, calls=%fused_computation.154 | convolution fusion | flops 4831838208 | bytes 17301504 | tf_op jit(solution)/shard_map/tf,td->fd/dot_general | solution.py:153
  488.9 2.8 copy.74
  491.7 8.6 multiply_convert_fusion.3
  500.5 2.8 copy.75
  503.3 2.5 convert_reduce_fusion.4
  505.9 40.1 %all-reduce.3 = (f32[2,768]{1,0:T(2,128)S(1)}, f32[7680]{0:T(1024)S(1)}) all-reduce(f32[2,768]{1,0:T(2,128)S(1)} %pad_maximum_fusion.3, f32[7680]{0:T(1024)S(1)} %constant_dynamic-update-slice_fusion), channel_id=6, replica_groups=mesh['dp'=32] {'dp'}, use_global_device_ids=true, to_apply=%region_20.21.clone | all-reduce | flops 9216 | bytes 73728
  549.0 99.9 %reduce-scatter.6.cloned.1.call-done = f32[24,2304]{1,0:T(8,128)} async-done(((f32[768,2304]{1,0:T(8,128)}), f32[24,2304]{1,0:T(8,128)}) %reduce-scatter.6.cloned.1.call-update) | async-done | bytes 221200 | tf_op jit(solution)/shard_map/reduce_scatter | solution.py:219
  650.8 139.4 %reduce-scatter.10.cloned.1.call-done = f32[24,3072]{1,0:T(8,128)} async-done(((f32[768,3072]{1,0:T(8,128)}), f32[24,3072]{1,0:T(8,128)}) %reduce-scatter.10.cloned.1.call-update) | async-done | bytes 294928 | tf_op jit(solution)/shard_map/reduce_scatter | solution.py:221
  792.1 140.1 %reduce-scatter.12.cloned.1.call-done = f32[96,768]{1,0:T(8,128)} async-done(((f32[3072,768]{1,0:T(8,128)}), f32[96,768]{1,0:T(8,128)}) %reduce-scatter.12.cloned.1.call-update) | async-done | bytes 294928 | tf_op jit(solution)/shard_map/reduce_scatter | solution.py:222
  (222 shorter events, 42.1 us)
Async XLA Ops:
  7.2 70.7 %copy-start.17 = (bf16[1024,768]{1,0:T(8,128)(2,1)S(1)}, bf16[1024,768]{1,0:T(8,128)(2,1)}, u32[]{:S(2)}) copy-start(bf16[1024,768]{1,0:T(8,128)(2,1)} %param.27) | copy-start | bytes 4718596
  7.2 77.5 %all-gather.5.cloned.1.call-start = ((), (), s32[]{:S(2)}) async-start(), calls=%async_computation.4 | async-start | bytes 3649536 | tf_op jit(solution)/shard_map/all_gather | solution.py:92
  9.0 171.4 %all-gather.7.cloned.1.call-start = ((), (), s32[]{:S(2)}) async-start(), calls=%async_computation.5 | async-start | bytes 1216512 | tf_op jit(solution)/shard_map/all_gather | solution.py:93
  10.6 186.6 %all-gather.9.cloned.1.call-start = ((), (), s32[]{:S(2)}) async-start(), calls=%async_computation.6 | async-start | bytes 4866048 | tf_op jit(solution)/shard_map/all_gather | solution.py:94
  12.3 250.6 %all-gather.11.cloned.1.call-start = ((), (), s32[]{:S(2)}) async-start(), calls=%async_computation.7 | async-start | bytes 4866048 | tf_op jit(solution)/shard_map/all_gather | solution.py:95
  13.0 12.9 %collective-permute-start = (bf16[2,24]{1,0:T(2,128)(2,1)S(1)}, bf16[2,24]{1,0:T(2,128)(2,1)S(1)}, u32[]{:S(2)}, u32[]{:S(2)}) collective-permute-start(bf16[2,24]{1,0:T(2,128)(2,1)S(1)} %convert_element_type.131), channel_id=1, source_target_pairs={{0,31},{1,0},{2,1},{3,2},{4,3},{5,4},{6,5},{7,6},{8,7},{9,8},{10,9... | collective-permute-start | bytes 296 | tf_op jit(solution)/shard_map/ppermute | solution.py:23
  21.0 526.4 %reduce-scatter.8.cloned.1.call-start = ((), (), s32[]{:S(2)}) async-start(), calls=%async_computation.9 | async-start | bytes 2433024 | tf_op jit(solution)/shard_map/reduce_scatter | solution.py:220
  25.9 139.2 %copy-start.5 = (pred[512,1024]{1,0:T(8,128)(4,1)}, pred[512,1024]{1,0:T(8,128)(4,1)S(1)}, u32[]{:S(2)}) copy-start(pred[512,1024]{1,0:T(8,128)(4,1)S(1)} %get-tuple-element.153) | copy-start | bytes 1572868
  26.0 3.5 collective-permute-start.1
  29.6 40.9 %collective-permute-start.2 = (bf16[2,96]{1,0:T(2,128)(2,1)S(1)}, bf16[2,96]{1,0:T(2,128)(2,1)S(1)}, u32[]{:S(2)}, u32[]{:S(2)}) collective-permute-start(bf16[2,96]{1,0:T(2,128)(2,1)S(1)} %pad_maximum_fusion.6), channel_id=1, source_target_pairs={{0,28},{1,29},{2,30},{3,31},{4,0},{5,1},{6,2},{7,3},{8,4},{9,5},{1... | collective-permute-start | bytes 1160 | tf_op jit(solution)/shard_map/ppermute | solution.py:23
  70.6 3.7 collective-permute-start.3
  74.4 9.5 %collective-permute-start.4 = (bf16[2,384]{1,0:T(2,128)(2,1)S(1)}, bf16[2,384]{1,0:T(2,128)(2,1)S(1)}, u32[]{:S(2)}, u32[]{:S(2)}) collective-permute-start(bf16[2,384]{1,0:T(2,128)(2,1)S(1)} %concatenate.41), channel_id=1, source_target_pairs={{0,16},{1,17},{2,18},{3,19},{4,20},{5,21},{6,22},{7,23},{8,24},{9,... | collective-permute-start | bytes 4616 | tf_op jit(solution)/shard_map/ppermute | solution.py:23
  77.3 103.1 %copy-start.49 = (f32[1,1024]{1,0:T(1,128)}, f32[1,1024]{1,0:T(1,128)S(1)}, u32[]{:S(2)}) copy-start(f32[1,1024]{1,0:T(1,128)S(1)} %convert_element_type.120) | copy-start | bytes 12292
  100.5 26.9 %copy-start.2 = (bf16[1024,2304]{0,1:T(8,128)(2,1)S(1)}, bf16[1024,2304]{0,1:T(8,128)(2,1)}, u32[]{:S(2)}) copy-start(bf16[1024,2304]{0,1:T(8,128)(2,1)} %copy.70) | copy-start | bytes 14155780
  115.1 16.2 %copy-start.1 = (f32[12,512,1024]{2,1,0:T(8,128)S(1)}, f32[12,512,1024]{2,1,0:T(8,128)}, u32[]{:S(2)}) copy-start(f32[12,512,1024]{2,1,0:T(8,128)} %get-tuple-element.160) | copy-start | bytes 75497472
  152.1 15.6 %copy-start = (f32[12,512,1024]{2,1,0:T(8,128)S(1)}, f32[12,512,1024]{2,1,0:T(8,128)}, u32[]{:S(2)}) copy-start(f32[12,512,1024]{2,1,0:T(8,128)} %get-tuple-element.162) | copy-start | bytes 75497472
  184.9 117.0 %copy-start.10 = (f32[1024,768]{0,1:T(8,128)}, f32[1024,768]{0,1:T(8,128)S(1)}, u32[]{:S(2)}) copy-start(f32[1024,768]{0,1:T(8,128)S(1)} %get-tuple-element.164) | copy-start | bytes 9437188
  185.0 12.2 %copy-start.44 = (f32[3072]{0:T(1024)S(1)}, f32[3072]{0:T(1024)}, u32[]{:S(2)}) copy-start(f32[3072]{0:T(1024)} %slice.120) | copy-start | bytes 36868
  185.0 12.2 %copy-start.45 = (f32[768]{0:T(1024)S(1)}, f32[768]{0:T(1024)}, u32[]{:S(2)}) copy-start(f32[768]{0:T(1024)} %get-tuple-element.149) | copy-start | bytes 9220
  197.1 65.8 %copy-start.47 = (f32[768]{0:T(1024)S(1)}, f32[768]{0:T(1024)}, u32[]{:S(2)}) copy-start(f32[768]{0:T(1024)} %get-tuple-element.148) | copy-start | bytes 9220
  275.9 18.9 %slice-start.2 = ((s8[4718592]{0:T(1024)(128)(4,1)}), s8[4194304]{0:T(1024)(128)(4,1)S(1)}, s32[]{:S(2)}) async-start(s8[4718592]{0:T(1024)(128)(4,1)} %bitcast.117), calls=%async_computation.14 | async-start | bytes 8388608
  279.4 15.4 %copy-start.22 = (bf16[1024,768]{0,1:T(8,128)(2,1)}, bf16[1024,768]{0,1:T(8,128)(2,1)S(1)}, u32[]{:S(2)}) copy-start(bf16[1024,768]{0,1:T(8,128)(2,1)S(1)} %get-tuple-element.139) | copy-start | bytes 4718596
  279.4 15.4 %slice-start.3 = ((s8[4718592]{0:T(1024)(128)(4,1)}), s8[524288]{0:T(1024)(128)(4,1)S(1)}, s32[]{:S(2)}) async-start(s8[4718592]{0:T(1024)(128)(4,1)} %bitcast.117), calls=%async_computation.15 | async-start | bytes 1048576
  309.7 34.6 %copy-start.15 = (bf16[512,768]{0,1:T(8,128)(2,1)}, bf16[512,768]{0,1:T(8,128)(2,1)S(1)}, u32[]{:S(2)}) copy-start(bf16[512,768]{0,1:T(8,128)(2,1)S(1)} %get-tuple-element.145) | copy-start | bytes 2359300
  324.0 20.3 %copy-start.6 = (pred[512,1024]{1,0:T(8,128)(4,1)S(1)}, pred[512,1024]{1,0:T(8,128)(4,1)}, u32[]{:S(2)}) copy-start(pred[512,1024]{1,0:T(8,128)(4,1)} %copy-done.5) | copy-start | bytes 1572868
  344.3 63.3 %slice-start = ((s8[4718592]{0:T(1024)(128)(4,1)}), s8[524288]{0:T(1024)(128)(4,1)S(1)}, s32[]{:S(2)}) async-start(s8[4718592]{0:T(1024)(128)(4,1)} %bitcast.97), calls=%async_computation.12 | async-start | bytes 1048576
  364.6 43.0 %slice-start.1 = ((s8[4718592]{0:T(1024)(128)(4,1)}), s8[4194304]{0:T(1024)(128)(4,1)S(1)}, s32[]{:S(2)}) async-start(s8[4718592]{0:T(1024)(128)(4,1)} %bitcast.97), calls=%async_computation.13 | async-start | bytes 8388608
  425.6 223.3 %reduce-scatter.6.cloned.1.call-start = ((), (), s32[]{:S(2)}) async-start(), calls=%async_computation.8 | async-start | bytes 7299072 | tf_op jit(solution)/shard_map/reduce_scatter | solution.py:219
  464.0 326.2 %reduce-scatter.10.cloned.1.call-start = ((), (), s32[]{:S(2)}) async-start(), calls=%async_computation.10 | async-start | bytes 9732096 | tf_op jit(solution)/shard_map/reduce_scatter | solution.py:221
  476.4 455.9 %reduce-scatter.12.cloned.1.call-start = ((), (), s32[]{:S(2)}) async-start(), calls=%async_computation.11 | async-start | bytes 9732096 | tf_op jit(solution)/shard_map/reduce_scatter | solution.py:222
  500.3 45.8 %copy-start.52 = (f32[2,24]{1,0:T(2,128)S(1)}, f32[2,24]{1,0:T(2,128)}, u32[]{:S(2)}) copy-start(f32[2,24]{1,0:T(2,128)} %param.32) | copy-start | bytes 580
  500.3 45.8 %copy-start.53 = (f32[2,24]{1,0:T(2,128)S(1)}, f32[2,24]{1,0:T(2,128)}, u32[]{:S(2)}) copy-start(f32[2,24]{1,0:T(2,128)} %param.44) | copy-start | bytes 580
  500.3 45.8 %copy-start.54 = (f32[2,24]{1,0:T(2,128)S(1)}, f32[2,24]{1,0:T(2,128)}, u32[]{:S(2)}) copy-start(f32[2,24]{1,0:T(2,128)} %param.38) | copy-start | bytes 580
  500.4 46.4 %copy-start.55 = (f32[240]{0:T(256)S(1)}, f32[240]{0:T(256)}, u32[]{:S(2)}) copy-start(f32[240]{0:T(256)} %param.33) | copy-start | bytes 2884
  500.4 46.4 %copy-start.56 = (f32[240]{0:T(256)S(1)}, f32[240]{0:T(256)}, u32[]{:S(2)}) copy-start(f32[240]{0:T(256)} %param.45) | copy-start | bytes 2884
  500.4 46.4 %copy-start.57 = (f32[240]{0:T(256)S(1)}, f32[240]{0:T(256)}, u32[]{:S(2)}) copy-start(f32[240]{0:T(256)} %param.39) | copy-start | bytes 2884
  500.4 47.1 %copy-start.27 = (f32[24,768]{1,0:T(8,128)S(1)}, f32[24,768]{1,0:T(8,128)}, u32[]{:S(2)}) copy-start(f32[24,768]{1,0:T(8,128)} %param.29) | copy-start | bytes 221188
  500.4 47.0 %copy-start.35 = (f32[24,768]{1,0:T(8,128)S(1)}, f32[24,768]{1,0:T(8,128)}, u32[]{:S(2)}) copy-start(f32[24,768]{1,0:T(8,128)} %param.41) | copy-start | bytes 221188
  500.4 47.0 %copy-start.36 = (f32[24,768]{1,0:T(8,128)S(1)}, f32[24,768]{1,0:T(8,128)}, u32[]{:S(2)}) copy-start(f32[24,768]{1,0:T(8,128)} %param.35) | copy-start | bytes 221188
  500.4 148.5 %copy-start.26 = (f32[24,2304]{1,0:T(8,128)S(1)}, f32[24,2304]{1,0:T(8,128)}, u32[]{:S(2)}) copy-start(f32[24,2304]{1,0:T(8,128)} %param.28) | copy-start | bytes 663556
  500.4 148.5 %copy-start.32 = (f32[24,2304]{1,0:T(8,128)S(1)}, f32[24,2304]{1,0:T(8,128)}, u32[]{:S(2)}) copy-start(f32[24,2304]{1,0:T(8,128)} %param.40) | copy-start | bytes 663556
  500.4 148.5 %copy-start.33 = (f32[24,2304]{1,0:T(8,128)S(1)}, f32[24,2304]{1,0:T(8,128)}, u32[]{:S(2)}) copy-start(f32[24,2304]{1,0:T(8,128)} %param.34) | copy-start | bytes 663556
  503.2 286.9 %copy-start.24 = (f32[24,3072]{1,0:T(8,128)S(1)}, f32[24,3072]{1,0:T(8,128)}, u32[]{:S(2)}) copy-start(f32[24,3072]{1,0:T(8,128)} %param.30) | copy-start | bytes 884740
  503.2 286.9 %copy-start.28 = (f32[24,3072]{1,0:T(8,128)S(1)}, f32[24,3072]{1,0:T(8,128)}, u32[]{:S(2)}) copy-start(f32[24,3072]{1,0:T(8,128)} %param.42) | copy-start | bytes 884740
  503.2 286.9 %copy-start.29 = (f32[24,3072]{1,0:T(8,128)S(1)}, f32[24,3072]{1,0:T(8,128)}, u32[]{:S(2)}) copy-start(f32[24,3072]{1,0:T(8,128)} %param.36) | copy-start | bytes 884740
  503.2 429.0 %copy-start.25 = (f32[96,768]{1,0:T(8,128)S(1)}, f32[96,768]{1,0:T(8,128)}, u32[]{:S(2)}) copy-start(f32[96,768]{1,0:T(8,128)} %param.31) | copy-start | bytes 884740
  503.3 429.0 %copy-start.30 = (f32[96,768]{1,0:T(8,128)S(1)}, f32[96,768]{1,0:T(8,128)}, u32[]{:S(2)}) copy-start(f32[96,768]{1,0:T(8,128)} %param.43) | copy-start | bytes 884740
  503.3 429.0 %copy-start.31 = (f32[96,768]{1,0:T(8,128)S(1)}, f32[96,768]{1,0:T(8,128)}, u32[]{:S(2)}) copy-start(f32[96,768]{1,0:T(8,128)} %param.37) | copy-start | bytes 884740
  (32 other events, 141.2 us)
Sparse Core Ops, SparseCore 0:
  11.5 63.1 all-gather.4
  78.2 52.8 all-gather.6
  134.5 62.5 all-gather.8
  200.5 62.4 all-gather.10
  425.8 97.8 reduce-scatter.7
  530.7 118.1 reduce-scatter.5
  655.4 134.7 reduce-scatter.9
  797.6 134.5 reduce-scatter.11
